TPU v7x, 32 devices: a whole 2x2x4 slice. The times are simulated.
32 devices in a mesh: seq: 4 (over z), head: 8 (over y, x, core).
Axes of the slice: x: 2, y: 2, z: 4, core: 2. Of those that a mesh axis runs over, the one named last changes fastest.
Arguments:
- x_in: bfloat16 [2048, 8192], P('seq', 'head'), may hold values from -6 to 6
- z_in: bfloat16 [2048, 8192], P('seq', 'head'), may hold values from -6 to 6
- bc_in: bfloat16 [2048, 2048], P('seq'), may hold values from -6 to 6
- conv_x: float32 [4, 8192], P(None, 'head'), may hold values from -3 to 3
- conv_bc: float32 [4, 2048], replicated, may hold values from -3 to 3
- dt: float32 [128, 2048], P('head', 'seq'), may hold values from 0 to 3, as said below
- a_log: float32 [128], P('head'), may hold values from -2 to 1, as said below
- skip_d: float32 [128], P('head'), may hold values from 0.5 to 1.5
- norm_gain: float32 [8192], P('head'), may hold values from 0.5 to 1.5
- seg_ids: int32 [2048], P('seq'), may hold values from 0 to 3, as said below
Outputs:
- mixed: bfloat16 [2048, 8192], P('seq', 'head')
Inputs may be any that keep to these rules, and one draw needn't show every extreme that they name: `a_log`: log of a decay rate of order one. `dt`: positive step sizes. `seg_ids`: document numbers never fall along the window, every document is nonempty, and the longest document holds exactly 1024 tokens.
All inputs are finite; a program needn't handle non-finite values.
Results may differ from a plain program's by a relative error of at most 0.0051.
Values may be sent and summed in bfloat16 or wider, within the bound.
No kernel may reach another device: no remote copies, remote signals or barrier semaphores. Data moves between devices by JAX's collectives and lax.ppermute only.
A program may use at most 64 MiB of HBM per device.

v0:
```python
import jax
import jax.numpy as jnp
from jax import lax
from jax.sharding import PartitionSpec as P

HEADS = 128
HEAD_DIM = 64
STATE = 128
GROUPS = 8
KERNEL = 4
SPAN = 128


def shifted(value, axis, steps):
    count = lax.axis_size(axis)
    first, last = (max(0, -steps), min(count, count - steps))
    return lax.ppermute(value, axis, [(source, source + steps) for source in range(first, last)])


def carried_in(x, axis, combine, identity):
    peers, place = (lax.axis_size(axis), lax.axis_index(axis))
    everything = jax.tree.map(
        lambda part, kind: lax.all_gather(part.astype(kind), axis), x, (jnp.bfloat16, jnp.bfloat16)
    )
    start = jax.tree.map(
        lambda part, zero: jnp.broadcast_to(jnp.asarray(zero, part.dtype), part.shape), x, identity
    )

    def hop(k, before):
        reached = k < place
        new = combine(
            before, jax.tree.map(lambda part, own: part[k].astype(own.dtype), everything, x)
        )
        return jax.tree.map(lambda a, b: jnp.where(reached, a, b), new, before)

    return lax.fori_loop(0, peers, hop, start)


def conv_silu(data, tail, weight, seg_float, tail_seg):
    rows = data.shape[0]
    padded = jnp.concatenate([tail, data], 0)
    seg_pad = jnp.concatenate([tail_seg.astype(jnp.float32), seg_float], 0)
    total = jnp.zeros(data.shape, jnp.float32)
    for offset in range(KERNEL):
        window = padded[offset : offset + rows].astype(jnp.float32)
        same_doc = (seg_pad[offset : offset + rows] == seg_float)[:, None]
        total = total + jnp.where(same_doc, window, 0.0) * weight[offset]
    return jax.nn.silu(total).astype(jnp.bfloat16)


def per_device(x_in, z_in, bc_in, conv_x, conv_bc, dt, a_log, skip_d, norm_gain, seg_ids):
    tok_rows = x_in.shape[0]
    local_heads = dt.shape[0]
    per_group = HEADS // GROUPS
    head_index = lax.axis_index("head")
    group = head_index * local_heads // per_group
    b_part = lax.dynamic_slice_in_dim(bc_in, group * STATE, STATE, 1)
    c_part = lax.dynamic_slice_in_dim(bc_in, GROUPS * STATE + group * STATE, STATE, 1)
    bc_mine = jnp.concatenate([b_part, c_part], 1)
    taps_b = lax.dynamic_slice_in_dim(conv_bc, group * STATE, STATE, 1)
    taps_c = lax.dynamic_slice_in_dim(conv_bc, GROUPS * STATE + group * STATE, STATE, 1)
    taps_mine = jnp.concatenate([taps_b, taps_c], 1)
    margin = KERNEL - 1
    tail_x, tail_bc, tail_seg = shifted(
        (
            x_in[tok_rows - margin :],
            bc_mine[tok_rows - margin :],
            seg_ids[tok_rows - margin :].astype(jnp.bfloat16),
        ),
        "seq",
        1,
    )
    seg_float = seg_ids.astype(jnp.float32)
    first_shard = lax.axis_index("seq") == 0
    tail_seg = jnp.where(first_shard, jnp.full(tail_seg.shape, -1.0, jnp.bfloat16), tail_seg)
    x_conv = conv_silu(x_in, tail_x, conv_x, seg_float, tail_seg)
    bc_conv = conv_silu(bc_mine, tail_bc, taps_mine, seg_float, tail_seg)
    prev_seg = tail_seg[margin - 1].astype(jnp.float32)
    spans = tok_rows // SPAN
    x_blocks = x_conv.reshape(spans, SPAN, local_heads, HEAD_DIM)
    b_blocks = bc_conv[:, :STATE].reshape(spans, SPAN, STATE)
    c_blocks = bc_conv[:, STATE:].reshape(spans, SPAN, STATE)
    dt_blocks = dt.reshape(local_heads, spans, SPAN).transpose(1, 0, 2)
    seg_blocks = seg_float.reshape(spans, SPAN)
    seg_before = jnp.concatenate([prev_seg[None], seg_blocks[:-1, -1]])
    rates = jnp.exp(a_log)
    log_decay = jnp.cumsum(-dt_blocks * rates[None, :, None], axis=2)
    causal = jnp.tril(jnp.ones((SPAN, SPAN), bool))
    same_doc = ((seg_blocks[:, :, None] == seg_blocks[:, None, :]) & causal[None])[:, None]
    spread = log_decay[:, :, :, None] - log_decay[:, :, None, :]
    decay = jnp.where(same_doc, jnp.exp(jnp.where(same_doc, spread, 0.0)), 0.0)
    scores = jnp.einsum("ctn,csn->cts", c_blocks, b_blocks, preferred_element_type=jnp.float32)
    weight_tensors = (scores[:, None] * decay * dt_blocks[:, :, None, :]).astype(jnp.bfloat16)
    y_diag = jnp.einsum(
        "chts,cshp->cthp", weight_tensors, x_blocks, preferred_element_type=jnp.float32
    )
    same_end = (seg_blocks == seg_blocks[:, -1:]).astype(jnp.float32)
    to_end = jnp.exp(log_decay[:, :, -1:] - log_decay) * dt_blocks * same_end[:, None, :]
    x_weighted = (x_blocks.astype(jnp.float32) * to_end.transpose(0, 2, 1)[..., None]).astype(
        jnp.bfloat16
    )
    fresh = jnp.einsum("cshp,csn->chpn", x_weighted, b_blocks, preferred_element_type=jnp.float32)
    keep = (
        jnp.exp(log_decay[:, :, -1])
        * (seg_blocks[:, -1] == seg_before).astype(jnp.float32)[:, None]
    )

    def local_step(carry, item):
        state, factor = carry
        keep_block, fresh_block = item
        return (
            (keep_block[:, None, None] * state + fresh_block, keep_block * factor),
            (state, factor),
        )

    zero_state = jnp.zeros((local_heads, HEAD_DIM, STATE), jnp.float32)
    (total_state, total_keep), (entering, factors) = lax.scan(
        local_step, (zero_state, jnp.ones((local_heads,), jnp.float32)), (keep, fresh)
    )

    def combine(earlier, later):
        return (earlier[0] * later[0], later[0][:, None, None] * earlier[1] + later[1])

    incoming = carried_in(
        (total_keep, total_state),
        "seq",
        combine,
        (jnp.ones_like(total_keep), jnp.zeros_like(total_state)),
    )[1]
    starts = entering + factors[:, :, None, None] * incoming[None]
    alive = (seg_blocks == seg_before[:, None]).astype(jnp.float32)
    y_carry = jnp.einsum(
        "ctn,chpn->cthp", c_blocks.astype(jnp.float32), starts, precision=lax.Precision.HIGHEST
    )
    y_carry = y_carry * (jnp.exp(log_decay).transpose(0, 2, 1) * alive[:, :, None])[..., None]
    summed = (y_diag + y_carry).reshape(tok_rows, local_heads, HEAD_DIM)
    summed = summed + skip_d[None, :, None] * x_conv.reshape(
        tok_rows, local_heads, HEAD_DIM
    ).astype(jnp.float32)
    gated = summed * jax.nn.silu(z_in.reshape(tok_rows, local_heads, HEAD_DIM).astype(jnp.float32))
    squares = jnp.sum(gated * gated, axis=(1, 2))
    gathered = lax.all_gather(squares[None], "head", axis=0, tiled=True)
    total_squares = jnp.sum(gathered, axis=0)
    mean_sq = total_squares / (HEADS * HEAD_DIM)
    normalized_output = (gated * lax.rsqrt(mean_sq + 1e-05)[:, None, None]).reshape(
        tok_rows, local_heads * HEAD_DIM
    )
    return (normalized_output * norm_gain).astype(jnp.bfloat16)


def solution(mesh):
    in_specs = (
        P("seq", "head"),
        P("seq", "head"),
        P("seq", None),
        P(None, "head"),
        P(),
        P("head", "seq"),
        P("head"),
        P("head"),
        P("head"),
        P("seq"),
    )
    out_specs = P("seq", "head")
    return jax.shard_map(
        per_device, mesh=mesh, in_specs=in_specs, out_specs=out_specs, check_vma=False
    )
```

profile of v0, /device:TPU:0, one launch (start us, length us, event | category | flops | bytes accessed | tf_op | source)
XLA Modules:
  0.0 97.1 jit_solution(2739810109216518925)
XLA Ops:
  6.5 0.0 all-gather.5.cloned.1.call-start
  6.6 1.0 %constant_dynamic-slice_fusion.4 = (bf16[512,128]{1,0:T(8,128)(2,1)S(1)}, bf16[512,128]{1,0:T(8,128)(2,1)S(1)}) fusion(bf16[512,2048]{1,0:T(8,128)(2,1)} %param.16, s32[]{:T(128)S(6)} %select_n.85, s32[]{:T(128)S(6)} %select_n.86), kind=kLoop, calls=%fused_computation.87 | loop fusion | bytes 524296 | tf_op jit(solution)/shard_map/dynamic_slice | solution.py:57
  7.6 5.0 %collective-permute-start.2 = (bf16[3,256]{1,0:T(4,128)(2,1)S(1)}, bf16[3,256]{1,0:T(4,128)(2,1)S(1)}, u32[]{:S(2)}, u32[]{:S(2)}) collective-permute-start(bf16[3,256]{1,0:T(4,128)(2,1)S(1)} %fusion.36), channel_id=1, source_target_pairs={{0,8},{8,16},{16,24},{1,9},{9,17},{17,25},{2,10},{10,18},{18,26},{... | collective-permute-start | bytes 4616 | tf_op jit(solution)/shard_map/ppermute | solution.py:17
  12.6 0.8 convert_bitcast_fusion
  13.4 0.1 slice.84
  13.4 3.5 %collective-permute-start = (bf16[3]{0:T(256)(128)(2,1)S(1)}, bf16[3]{0:T(256)(128)(2,1)S(1)}, u32[]{:S(2)}, u32[]{:S(2)}) collective-permute-start(bf16[3]{0:T(256)(128)(2,1)S(1)} %slice.84), channel_id=1, source_target_pairs={{0,8},{8,16},{16,24},{1,9},{9,17},{17,25},{2,10},{10,18},{18,26},{... | collective-permute-start | bytes 26 | tf_op jit(solution)/shard_map/ppermute | solution.py:17
  16.9 0.7 slice.86
  17.6 0.2 copy.69
  17.8 3.5 %collective-permute-start.1 = (bf16[3,1024]{0,1:T(8,128)(2,1)S(1)}, bf16[3,1024]{0,1:T(8,128)(2,1)S(1)}, u32[]{:S(2)}, u32[]{:S(2)}) collective-permute-start(bf16[3,1024]{0,1:T(8,128)(2,1)S(1)} %copy.69), channel_id=1, source_target_pairs={{0,8},{8,16},{16,24},{1,9},{9,17},{17,25},{2,10},{10,18},{18,26},{... | collective-permute-start | bytes 18440 | tf_op jit(solution)/shard_map/ppermute | solution.py:17
  21.4 1.5 %copy.70 = bf16[512,1024]{0,1:T(8,128)(2,1)S(1)} copy(bf16[512,1024]{1,0:T(8,128)(2,1)} %param.14) | data formatting | bytes 2097152 | tf_op args[0]
  22.9 0.7 constant_dynamic-slice_fusion.2
  23.6 0.2 slice_reduce_fusion.2
  23.8 0.1 negate_multiply_fusion
  23.9 1.1 %reduce_window_sum.11 = f32[4,16,128]{2,1,0:T(8,128)S(1)} reduce-window(f32[4,16,128]{2,1,0:T(8,128)S(1)} %negate_multiply_fusion, f32[]{:T(128)} %constant.81.clone.1), window={size=1x1x128 pad=0_0x0_0x127_0}, to_apply=%region_0.1 | reduce-window | flops 1040384 | bytes 65540 | tf_op jit(solution)/shard_map/jit(cumsum)/reduce_window_sum | solution.py:87
  25.0 0.2 slice_reduce_fusion
  25.2 0.1 pad_maximum_fusion.2
  25.3 0.1 slice_compare_fusion.2
  25.4 0.6 slice.108
  26.6 0.1 pad_maximum_fusion.4
  26.7 0.2 slice_reduce_fusion.1
  26.9 0.1 compare_convert_fusion
  27.0 0.1 fusion.35
  27.1 0.1 exponential_multiply_fusion
  27.1 0.1 maximum_maximum_fusion
  27.2 0.7 multiply_convert_fusion.3
  28.0 2.5 %multiply_convert_fusion.2 = bf16[512,1024]{0,1:T(8,128)(2,1)S(1)} fusion(bf16[512,1024]{0,1:T(8,128)(2,1)S(1)} %copy.70, bf16[3,1024]{0,1:T(8,128)(2,1)S(1)} %collective-permute-done.1, f32[1024]{0:T(1024)S(1)} %bitcast.111, f32[1024]{0:T(1024)S(1)} %bitcast.112, f32[1024]{0:T(1024)S(1)} %bitcast.110, f32[1024]{0:T(1024)S(1)} %bitcast.109, ...), kind=kLoop, calls=%fused_computation.33 | loop fusion | flops 15204352 | bytes 2121728 | tf_op jit(solution)/shard_map/convert_element_type | solution.py:48
  30.6 1.3 %reshape.117 = bf16[4,128,16,64]{1,0,3,2:T(4,128)(2,1)} reshape(bf16[512,1024]{0,1:T(8,128)(2,1)S(1)} %multiply_convert_fusion.2) | data formatting | bytes 2097152 | tf_op jit(solution)/shard_map/reshape | solution.py:80
  31.8 0.0 copy-done.1
  31.9 1.6 %fusion.27 = f32[4,16,64,128]{3,2,1,0:T(8,128)S(1)} fusion(bf16[4,128,128,1]{2,1,3,0:T(8,128)(2,1)S(1)} %bitcast.105, f32[4,128,16]{1,2,0:T(8,128)S(1)} %fusion.35, bf16[4,128,16,64]{1,0,3,2:T(4,128)(2,1)} %reshape.117), kind=kOutput, calls=%fused_computation.41 | convolution fusion | flops 135790592 | bytes 3309568 | tf_op jit(solution)/shard_map/cshp,csn->chpn/dot_general | solution.py:102
  33.5 4.1 %while.31 = (s32[]{:T(128)}, f32[16,64,128]{2,1,0:T(8,128)S(1)}, f32[16]{0:T(128)S(1)}, f32[4,16,64,128]{3,2,1,0:T(8,128)}, f32[4,16]{1,0:T(4,128)S(1)}, /*index...) while((s32[]{:T(128)}, f32[16,64,128]{2,1,0:T(8,128)S(1)}, ...), condition=%wide.region_2.3_spmd.clone, body=%wide.region_1.2_spmd.clone.sunk | while | flops 524323 | bytes 2622581 | solution.py:117
  33.6 0.8 bitcast_dynamic-update-slice_fusion.2
  34.4 0.1 bitcast_add_fusion.4
  34.6 0.8 bitcast_dynamic-update-slice_fusion.2
  35.4 0.1 bitcast_add_fusion.4
  35.6 0.9 bitcast_dynamic-update-slice_fusion.2
  36.5 0.1 bitcast_add_fusion.4
  36.7 0.8 bitcast_dynamic-update-slice_fusion.2
  37.5 0.1 bitcast_add_fusion.4
  37.6 0.8 convert_element_type.134
  38.4 0.0 all-gather.5.cloned.1.call-update
  38.5 1.5 %copy.77 = bf16[512,1024]{0,1:T(8,128)(2,1)S(1)} copy(bf16[512,1024]{1,0:T(8,128)(2,1)} %param.15) | data formatting | bytes 2097152 | tf_op args[1]
  40.0 0.0 copy-start.7
  40.0 0.0 copy-start.9
  40.0 1.7 %reshape.125 = f32[4,128,16,64]{1,0,3,2:T(4,128)} reshape(bf16[512,1024]{0,1:T(8,128)(2,1)S(1)} %copy.77) | data formatting | bytes 3145728 | tf_op jit(solution)/shard_map/convert_element_type | solution.py:140
  41.7 0.1 mul.327
  41.8 0.1 mul.328
  41.9 0.7 dynamic-slice
  43.2 0.1 compare_and_fusion
  43.4 0.2 fusion.45
  43.6 0.2 dynamic-update-slice
  43.9 9.7 %all-reduce = bf16[64]{0:T(256)(128)(2,1)S(1)} all-reduce(bf16[64]{0:T(256)(128)(2,1)S(1)} %dynamic-update-slice), channel_id=2, replica_groups=mesh['seq'=4,'head'=8] {'seq'}, use_global_device_ids=true, to_apply=%add | all-reduce | flops 64 | bytes 256
  53.6 0.1 reshape.126
  53.6 3.2 %fusion.4 = f32[4,16,64,128]{3,2,1,0:T(8,128)} fusion(f32[4,16,128]{2,1,0:T(8,128)S(1)} %bitcast_bitcast_fusion.1, f32[4,16,128]{2,1,0:T(8,128)S(1)} %reduce_window_sum.11, f32[4,128,128]{2,1,0:T(8,128)S(1)} %fusion.45, pred[4,128,128]{2,1,0:T(8,128)(4,1)S(1)} %compare_and_fusion, bf16[4,128,16,64]{1,0,3,2:T(4,128)(2,1)S(1)} %copy-done.3), kind=kOutput, calls=%fused_computation.13 | convolution fusion | flops 140509184 | bytes 3538944 | tf_op jit(solution)/shard_map/chts,cshp->cthp/dot_general | solution.py:94
  56.8 8.5 %all-gather.5.cloned.1.call-done = bf16[64,64,128]{2,1,0:T(8,128)(2,1)} async-done(((bf16[16,64,128]{2,1,0:T(8,128)(2,1)}), bf16[64,64,128]{2,1,0:T(8,128)(2,1)}) %all-gather.5.cloned.1.call-update) | async-done | bytes 1048592 | tf_op jit(solution)/shard_map/all_gather | solution.py:23
  65.3 4.5 %while.32 = (s32[]{:T(128)}, f32[16,64,128]{2,1,0:T(8,128)S(1)}, s32[]{:T(128)}, bf16[4,16]{1,0:T(4,128)(2,1)S(1)}, bf16[4,16,64,128]{3,2,1,0:T(8,128)(2,1)}, /*index=5*/s32[]{:T(128)}, s32[]{:T(128)}) while((s32[]{:T(128)}, f32[16,64,128]{2,1,0:T(8,128)S(1)}, s32[]{:T(128)}, bf16[4,16]{1,0:T(4,128)(2,1)S(1)}, ...), condition=%wide.region_4.5_spmd.clone, body=%wide.region_3.4_spmd.clone.sunk | while | flops 655380 | bytes 1310985 | solution.py:36
  65.3 1.1 %fusion.56 = f32[16,64,128]{2,1,0:T(8,128)S(1)} fusion(f32[16,64,128]{2,1,0:T(8,128)S(1)} %get-tuple-element.359, bf16[4,16,64,128]{3,2,1,0:T(8,128)(2,1)} %get-tuple-element.369, s32[]{:T(128)} %get-tuple-element.358, f32[16]{0:T(128)S(1)} %bitcast_convert_fusion.2, pred[]{:T(512)S(6)} %compare.9, pred[]{:T(512)S(6)} %lt.37), kind=kLoop, calls=%fused_computation.8.clone.1 | loop fusion | flops 655360 | bytes 1310790 | tf_op jit(solution)/shard_map/while/body/eval_jaxpr/jit(_where)/select_n | solution.py:34
  66.4 1.1 %fusion.56 = f32[16,64,128]{2,1,0:T(8,128)S(1)} fusion(f32[16,64,128]{2,1,0:T(8,128)S(1)} %get-tuple-element.359, bf16[4,16,64,128]{3,2,1,0:T(8,128)(2,1)} %get-tuple-element.369, s32[]{:T(128)} %get-tuple-element.358, f32[16]{0:T(128)S(1)} %bitcast_convert_fusion.2, pred[]{:T(512)S(6)} %compare.9, pred[]{:T(512)S(6)} %lt.37), kind=kLoop, calls=%fused_computation.8.clone.1 | loop fusion | flops 655360 | bytes 1310790 | tf_op jit(solution)/shard_map/while/body/eval_jaxpr/jit(_where)/select_n | solution.py:34
  67.5 1.1 %fusion.56 = f32[16,64,128]{2,1,0:T(8,128)S(1)} fusion(f32[16,64,128]{2,1,0:T(8,128)S(1)} %get-tuple-element.359, bf16[4,16,64,128]{3,2,1,0:T(8,128)(2,1)} %get-tuple-element.369, s32[]{:T(128)} %get-tuple-element.358, f32[16]{0:T(128)S(1)} %bitcast_convert_fusion.2, pred[]{:T(512)S(6)} %compare.9, pred[]{:T(512)S(6)} %lt.37), kind=kLoop, calls=%fused_computation.8.clone.1 | loop fusion | flops 655360 | bytes 1310790 | tf_op jit(solution)/shard_map/while/body/eval_jaxpr/jit(_where)/select_n | solution.py:34
  68.7 1.1 %fusion.56 = f32[16,64,128]{2,1,0:T(8,128)S(1)} fusion(f32[16,64,128]{2,1,0:T(8,128)S(1)} %get-tuple-element.359, bf16[4,16,64,128]{3,2,1,0:T(8,128)(2,1)} %get-tuple-element.369, s32[]{:T(128)} %get-tuple-element.358, f32[16]{0:T(128)S(1)} %bitcast_convert_fusion.2, pred[]{:T(512)S(6)} %compare.9, pred[]{:T(512)S(6)} %lt.37), kind=kLoop, calls=%fused_computation.8.clone.1 | loop fusion | flops 655360 | bytes 1310790 | tf_op jit(solution)/shard_map/while/body/eval_jaxpr/jit(_where)/select_n | solution.py:34
  69.8 4.9 %fusion.9 = (f32[4,128]{1,0:T(4,128)S(1)}, f32[4,128,16,64]{1,3,2,0:T(8,128)S(1)}) fusion(f32[4,128,16,64]{1,0,3,2:T(4,128)} %reshape.125, f32[16]{0:T(128)S(1)} %copy-done.7, bf16[4,128,16,64]{1,0,3,2:T(4,128)(2,1)S(1)} %copy-done.3, f32[4,128,16]{1,2,0:T(8,128)S(1)} %multiply_bitcast_fusion, bf16[4,128,128,1]{2,1,3,0:T(8,128)(2,1)S(1)} %bitcast.108, ...), kind=kOutput, calls=%fused_computation.18 | convolution fusion | flops 812645888 | bytes 10127680 | tf_op jit(solution)/shard_map/ctn,chpn->cthp/dot_general | solution.py:132
  74.7 2.8 %copy.76 = f32[4,128,16,64]{1,0,3,2:T(4,128)} copy(f32[4,128,16,64]{1,3,2,0:T(8,128)S(1)} %get-tuple-element.243) | data formatting | bytes 4194304 | tf_op jit(solution)/shard_map/add | solution.py:136
  77.5 8.9 %all-gather.2 = f32[8,1,512]{2,1,0:T(1,128)S(1)} all-gather(f32[1,1,512]{2,1,0:T(1,128)S(1)} %bitcast.117), channel_id=1, replica_groups=mesh['seq'=4,'head'=8] {'head'}, dimensions={0}, use_global_device_ids=true | all-gather | bytes 18432 | tf_op jit(solution)/shard_map/all_gather | solution.py:142
  86.4 2.5 %fusion.13 = bf16[512,1024]{0,1:T(8,128)(2,1)S(1)} fusion(f32[128,8,4,128]{3,2,1,0:T(4,128)} %bitcast.103, bf16[512,1024]{0,1:T(8,128)(2,1)S(1)} %copy-done.2, f32[1024]{0:T(1024)S(1)} %copy-done.6, f32[512]{0:T(512)S(1)} %add_rsqrt_fusion, f32[1024]{0:T(1024)S(1)} %mul.328, bf16[512,1024]{0,1:T(8,128)(2,1)S(1)} %copy.77), kind=kLoop, calls=%fused_computation.23 | loop fusion | flops 6291456 | bytes 5253120 | tf_op jit(solution)/shard_map/convert_element_type | solution.py:148
  88.9 1.3 %copy.80 = bf16[512,1024]{1,0:T(8,128)(2,1)} copy(bf16[512,1024]{0,1:T(8,128)(2,1)S(1)} %fusion.13) | data formatting | bytes 2097152 | tf_op jit(solution)/shard_map/convert_element_type | solution.py:148
  (50 shorter events, 0.5 us)
Async XLA Ops:
  6.5 17.3 %copy-start = (f32[16,512]{1,0:T(8,128)S(1)}, f32[16,512]{1,0:T(8,128)}, u32[]{:S(2)}) copy-start(f32[16,512]{1,0:T(8,128)} %param.19) | copy-start | bytes 98308
  6.5 18.8 %copy-start.4 = (s32[512]{0:T(512)S(1)}, s32[512]{0:T(512)}, u32[]{:S(2)}) copy-start(s32[512]{0:T(512)} %param.23) | copy-start | bytes 6148
  6.5 17.1 %copy-start.5 = (f32[4,1024]{1,0:T(4,128)S(1)}, f32[4,1024]{1,0:T(4,128)}, u32[]{:S(2)}) copy-start(f32[4,1024]{1,0:T(4,128)} %param.17) | copy-start | bytes 49156
  6.5 17.1 %copy-start.8 = (f32[16]{0:T(128)S(1)}, f32[16]{0:T(128)}, u32[]{:S(2)}) copy-start(f32[16]{0:T(128)} %param.20) | copy-start | bytes 196
  6.5 58.7 %all-gather.5.cloned.1.call-start = ((), (), s32[]{:S(2)}) async-start(), calls=%async_computation | async-start | bytes 1310720 | tf_op jit(solution)/shard_map/all_gather | solution.py:23
  7.6 19.5 %collective-permute-start.2 = (bf16[3,256]{1,0:T(4,128)(2,1)S(1)}, bf16[3,256]{1,0:T(4,128)(2,1)S(1)}, u32[]{:S(2)}, u32[]{:S(2)}) collective-permute-start(bf16[3,256]{1,0:T(4,128)(2,1)S(1)} %fusion.36), channel_id=1, source_target_pairs={{0,8},{8,16},{16,24},{1,9},{9,17},{17,25},{2,10},{10,18},{18,26},{... | collective-permute-start | bytes 4616 | tf_op jit(solution)/shard_map/ppermute | solution.py:17
  13.4 11.8 %collective-permute-start = (bf16[3]{0:T(256)(128)(2,1)S(1)}, bf16[3]{0:T(256)(128)(2,1)S(1)}, u32[]{:S(2)}, u32[]{:S(2)}) collective-permute-start(bf16[3]{0:T(256)(128)(2,1)S(1)} %slice.84), channel_id=1, source_target_pairs={{0,8},{8,16},{16,24},{1,9},{9,17},{17,25},{2,10},{10,18},{18,26},{... | collective-permute-start | bytes 26 | tf_op jit(solution)/shard_map/ppermute | solution.py:17
  17.8 10.1 %collective-permute-start.1 = (bf16[3,1024]{0,1:T(8,128)(2,1)S(1)}, bf16[3,1024]{0,1:T(8,128)(2,1)S(1)}, u32[]{:S(2)}, u32[]{:S(2)}) collective-permute-start(bf16[3,1024]{0,1:T(8,128)(2,1)S(1)} %copy.69), channel_id=1, source_target_pairs={{0,8},{8,16},{16,24},{1,9},{9,17},{17,25},{2,10},{10,18},{18,26},{... | collective-permute-start | bytes 18440 | tf_op jit(solution)/shard_map/ppermute | solution.py:17
  30.6 1.3 %copy-start.1 = (bf16[512,1024]{0,1:T(8,128)(2,1)}, bf16[512,1024]{0,1:T(8,128)(2,1)S(1)}, u32[]{:S(2)}) copy-start(bf16[512,1024]{0,1:T(8,128)(2,1)S(1)} %multiply_convert_fusion.2) | copy-start | bytes 3145732
  40.0 1.8 %copy-start.7 = (f32[16]{0:T(128)S(1)}, f32[16]{0:T(128)}, u32[]{:S(2)}) copy-start(f32[16]{0:T(128)} %param.21) | copy-start | bytes 196
  40.0 1.9 %copy-start.9 = (u32[32]{0:T(128)S(1)}, u32[32]{0:T(128)}, u32[]{:S(2)}) copy-start(u32[32]{0:T(128)} %constant.97) | copy-start | bytes 388
  40.0 13.6 %copy-start.3 = (bf16[4,128,16,64]{1,0,3,2:T(4,128)(2,1)S(1)}, bf16[4,128,16,64]{1,0,3,2:T(4,128)(2,1)}, u32[]{:S(2)}) copy-start(bf16[4,128,16,64]{1,0,3,2:T(4,128)(2,1)} %reshape.117) | copy-start | bytes 3145732
  74.7 11.7 %copy-start.2 = (bf16[512,1024]{0,1:T(8,128)(2,1)S(1)}, bf16[512,1024]{0,1:T(8,128)(2,1)}, u32[]{:S(2)}) copy-start(bf16[512,1024]{0,1:T(8,128)(2,1)} %copy-done.1) | copy-start | bytes 3145732
  74.7 11.7 %copy-start.6 = (f32[1024]{0:T(1024)S(1)}, f32[1024]{0:T(1024)}, u32[]{:S(2)}) copy-start(f32[1024]{0:T(1024)} %param.22) | copy-start | bytes 12292
Sparse Core Ops, SparseCore 0:
  38.6 26.6 all-gather.4
where the time goes:
time: 97.6 us; the launch traced here: 97.1 us
  blocking collectives  18.5 us (19%)
  other arithmetic  17.8 us (18%)
  local copies, waits for them, and re-layouts  15.1 us (15%)
  between operations  15.1 us (15%)
  starting transfers between devices  12 us (12%)
  matrix products  9.94 us (10%)
  waiting for transfers between devices  8.49 us (9%)
    ppermute x3, starting transfers between devices, shifted(): lax.ppermute(value, axis, [(source, source + steps) for source in range(f...  11.9 us
    unnamed x1, blocking collectives  9.67 us
    all_gather x1, blocking collectives, per_device(): gathered = lax.all_gather(squares[None], 'head', axis=0, tiled=True)  8.86 us
    all_gather x1, waiting for transfers between devices, carried_in(): lax.all_gather(part.astype(kind), axis)  8.46 us
    dot_general x1, matrix products, per_device(): jnp.einsum('ctn,chpn->cthp', c_blocks.astype(jnp.float32), starts, precis...  4.94 us
    select_n x4, other arithmetic, hop(): return jax.tree.map(lambda a, b: jnp.where(reached, a, b), new, before)  4.36 us
    unnamed x25, local copies, waits for them, and re-layouts  3.98 us
    dynamic_update_slice x4, other arithmetic, per_device(): lax.scan(local_step, (zero_state, jnp.ones((local_heads,), jnp.float32)),...  3.37 us
  transfers between devices with their start and end apart: 4, of which 1 were waited for; matrix products, arithmetic and copies ran while one was open for 16% of the time, Pallas kernels for 0%

commit v1 on v0

--- a/solution.py
+++ b/solution.py
@@ -139,7 +139,9 @@
     ).astype(jnp.float32)
     gated = summed * jax.nn.silu(z_in.reshape(tok_rows, local_heads, HEAD_DIM).astype(jnp.float32))
     squares = jnp.sum(gated * gated, axis=(1, 2))
-    gathered = lax.all_gather(squares[None], "head", axis=0, tiled=True)
+    gathered = jnp.concatenate(
+        lax.all_to_all(jnp.stack([squares[None]] * lax.axis_size("head")), "head", 0, 0), axis=0
+    )
     total_squares = jnp.sum(gathered, axis=0)
     mean_sq = total_squares / (HEADS * HEAD_DIM)
     normalized_output = (gated * lax.rsqrt(mean_sq + 1e-05)[:, None, None]).reshape(

time: 97.6 us -> 96.3 us (0.987)
  blocking collectives: 18.5 us -> 9.63 us
  starting transfers between devices: 12 us -> 15.6 us
  local copies, waits for them, and re-layouts: 15.1 us -> 17.4 us
  matrix products: 9.94 us -> 11.2 us
    all_gather x1 -> x0, blocking collectives: 8.86 us -> none  [per_device(): gathered = lax.all_gather(squares[None], 'head', axis=0, tiled=True)]
    all_to_all x0 -> x1, starting transfers between devices: none -> 3.65 us  [per_device(): lax.all_to_all(jnp.stack([squares[None]] * lax.axis_size('head')), 'head'...]
    add x1, local copies, waits for them, and re-layouts: 2.76 us -> 4.42 us  [per_device(): summed = (y_diag + y_carry).reshape(tok_rows, local_heads, HEAD_DIM)]
    dot_general x1, matrix products: 4.94 us -> 6.21 us  [per_device(): jnp.einsum('ctn,chpn->cthp', c_blocks.astype(jnp.float32), starts, precis...]
  transfers between devices with their start and end apart: 4 -> 5, of which waited for: 1 -> 2; matrix products, arithmetic and copies ran while one was open for 16% -> 21% of each run, Pallas kernels for 0% -> 0%
where the time goes in v1:
time: 96.3 us; the launch traced here: 95.7 us
  other arithmetic  17.8 us (18%)
  local copies, waits for them, and re-layouts  17.4 us (18%)
  starting transfers between devices  15.6 us (16%)
  between operations  15 us (16%)
  matrix products  11.2 us (12%)
  blocking collectives  9.63 us (10%)
  waiting for transfers between devices  8.9 us (9%)
    ppermute x3, starting transfers between devices, shifted(): lax.ppermute(value, axis, [(source, source + steps) for source in range(f...  11.9 us
    unnamed x1, blocking collectives  9.63 us
    all_gather x1, waiting for transfers between devices, carried_in(): lax.all_gather(part.astype(kind), axis)  8.7 us
    dot_general x1, matrix products, per_device(): jnp.einsum('ctn,chpn->cthp', c_blocks.astype(jnp.float32), starts, precis...  6.21 us
    add x1, local copies, waits for them, and re-layouts, per_device(): summed = (y_diag + y_carry).reshape(tok_rows, local_heads, HEAD_DIM)  4.42 us
    select_n x4, other arithmetic, hop(): return jax.tree.map(lambda a, b: jnp.where(reached, a, b), new, before)  4.37 us
    unnamed x25, local copies, waits for them, and re-layouts  3.97 us
    all_to_all x1, starting transfers between devices, per_device(): lax.all_to_all(jnp.stack([squares[None]] * lax.axis_size('head')), 'head'...  3.65 us
  transfers between devices with their start and end apart: 5, of which 2 were waited for; matrix products, arithmetic and copies ran while one was open for 21% of the time, Pallas kernels for 0%

profile of v1, /device:TPU:0, one launch (start us, length us, event | category | flops | bytes accessed | tf_op | source)
XLA Modules:
  0.0 95.7 jit_solution(6209515698445915901)
XLA Ops:
  6.5 0.0 all-gather.4.cloned.1.call-start
  6.6 1.0 %constant_dynamic-slice_fusion.4 = (bf16[512,128]{1,0:T(8,128)(2,1)S(1)}, bf16[512,128]{1,0:T(8,128)(2,1)S(1)}) fusion(bf16[512,2048]{1,0:T(8,128)(2,1)} %param.16, s32[]{:T(128)S(6)} %select_n.85, s32[]{:T(128)S(6)} %select_n.86), kind=kLoop, calls=%fused_computation.87 | loop fusion | bytes 524296 | tf_op jit(solution)/shard_map/dynamic_slice | solution.py:57
  7.6 5.0 %collective-permute-start.2 = (bf16[3,256]{1,0:T(4,128)(2,1)S(1)}, bf16[3,256]{1,0:T(4,128)(2,1)S(1)}, u32[]{:S(2)}, u32[]{:S(2)}) collective-permute-start(bf16[3,256]{1,0:T(4,128)(2,1)S(1)} %fusion.36), channel_id=1, source_target_pairs={{0,8},{8,16},{16,24},{1,9},{9,17},{17,25},{2,10},{10,18},{18,26},{... | collective-permute-start | bytes 4616 | tf_op jit(solution)/shard_map/ppermute | solution.py:17
  12.6 0.8 convert_bitcast_fusion
  13.4 0.1 slice.84
  13.4 3.5 %collective-permute-start = (bf16[3]{0:T(256)(128)(2,1)S(1)}, bf16[3]{0:T(256)(128)(2,1)S(1)}, u32[]{:S(2)}, u32[]{:S(2)}) collective-permute-start(bf16[3]{0:T(256)(128)(2,1)S(1)} %slice.84), channel_id=1, source_target_pairs={{0,8},{8,16},{16,24},{1,9},{9,17},{17,25},{2,10},{10,18},{18,26},{... | collective-permute-start | bytes 26 | tf_op jit(solution)/shard_map/ppermute | solution.py:17
  16.9 0.7 slice.86
  17.6 0.2 copy.83
  17.8 3.5 %collective-permute-start.1 = (bf16[3,1024]{0,1:T(8,128)(2,1)S(1)}, bf16[3,1024]{0,1:T(8,128)(2,1)S(1)}, u32[]{:S(2)}, u32[]{:S(2)}) collective-permute-start(bf16[3,1024]{0,1:T(8,128)(2,1)S(1)} %copy.83), channel_id=1, source_target_pairs={{0,8},{8,16},{16,24},{1,9},{9,17},{17,25},{2,10},{10,18},{18,26},{... | collective-permute-start | bytes 18440 | tf_op jit(solution)/shard_map/ppermute | solution.py:17
  21.4 1.5 %copy.84 = bf16[512,1024]{0,1:T(8,128)(2,1)S(1)} copy(bf16[512,1024]{1,0:T(8,128)(2,1)} %param.14) | data formatting | bytes 2097152 | tf_op args[0]
  22.9 0.7 constant_dynamic-slice_fusion.2
  23.6 0.2 slice_reduce_fusion.2
  23.8 0.1 negate_multiply_fusion
  23.9 1.1 %reduce_window_sum.11 = f32[4,16,128]{2,1,0:T(8,128)S(1)} reduce-window(f32[4,16,128]{2,1,0:T(8,128)S(1)} %negate_multiply_fusion, f32[]{:T(128)} %constant.81.clone.1), window={size=1x1x128 pad=0_0x0_0x127_0}, to_apply=%region_0.1 | reduce-window | flops 1040384 | bytes 65540 | tf_op jit(solution)/shard_map/jit(cumsum)/reduce_window_sum | solution.py:87
  25.0 0.2 slice_reduce_fusion
  25.2 0.1 pad_maximum_fusion.2
  25.3 0.1 slice_compare_fusion.2
  25.4 0.6 slice.108
  26.6 0.1 pad_maximum_fusion.4
  26.7 0.2 slice_reduce_fusion.1
  26.9 0.1 compare_convert_fusion
  27.0 0.1 fusion.35
  27.1 0.1 exponential_multiply_fusion
  27.1 0.1 maximum_maximum_fusion
  27.2 0.7 multiply_convert_fusion.3
  28.0 2.5 %multiply_convert_fusion.2 = bf16[512,1024]{0,1:T(8,128)(2,1)S(1)} fusion(bf16[512,1024]{0,1:T(8,128)(2,1)S(1)} %copy.84, bf16[3,1024]{0,1:T(8,128)(2,1)S(1)} %collective-permute-done.1, f32[1024]{0:T(1024)S(1)} %bitcast.111, f32[1024]{0:T(1024)S(1)} %bitcast.112, f32[1024]{0:T(1024)S(1)} %bitcast.110, f32[1024]{0:T(1024)S(1)} %bitcast.109, ...), kind=kLoop, calls=%fused_computation.33 | loop fusion | flops 15204352 | bytes 2121728 | tf_op jit(solution)/shard_map/convert_element_type | solution.py:48
  30.6 1.3 %reshape.122 = bf16[4,128,16,64]{1,0,3,2:T(4,128)(2,1)} reshape(bf16[512,1024]{0,1:T(8,128)(2,1)S(1)} %multiply_convert_fusion.2) | data formatting | bytes 2097152 | tf_op jit(solution)/shard_map/reshape | solution.py:80
  31.8 0.0 copy-done.1
  31.9 1.6 %fusion.27 = f32[4,16,64,128]{3,2,1,0:T(8,128)S(1)} fusion(bf16[4,128,128,1]{2,1,3,0:T(8,128)(2,1)S(1)} %bitcast.105, f32[4,128,16]{1,2,0:T(8,128)S(1)} %fusion.35, bf16[4,128,16,64]{1,0,3,2:T(4,128)(2,1)} %reshape.122), kind=kOutput, calls=%fused_computation.41 | convolution fusion | flops 135790592 | bytes 3309568 | tf_op jit(solution)/shard_map/cshp,csn->chpn/dot_general | solution.py:102
  33.5 4.1 %while.31 = (s32[]{:T(128)}, f32[16,64,128]{2,1,0:T(8,128)S(1)}, f32[16]{0:T(128)S(1)}, f32[4,16,64,128]{3,2,1,0:T(8,128)}, f32[4,16]{1,0:T(4,128)S(1)}, /*index...) while((s32[]{:T(128)}, f32[16,64,128]{2,1,0:T(8,128)S(1)}, ...), condition=%wide.region_2.3_spmd.clone, body=%wide.region_1.2_spmd.clone.sunk | while | flops 524323 | bytes 2622581 | solution.py:117
  33.6 0.9 bitcast_dynamic-update-slice_fusion.2
  34.4 0.1 bitcast_add_fusion.4
  34.6 0.8 bitcast_dynamic-update-slice_fusion.2
  35.4 0.1 bitcast_add_fusion.4
  35.6 0.9 bitcast_dynamic-update-slice_fusion.2
  36.5 0.1 bitcast_add_fusion.4
  36.7 0.8 bitcast_dynamic-update-slice_fusion.2
  37.5 0.1 bitcast_add_fusion.4
  37.7 0.8 convert_element_type.134
  38.4 0.0 all-gather.4.cloned.1.call-update
  38.5 1.5 %copy.91 = bf16[512,1024]{0,1:T(8,128)(2,1)S(1)} copy(bf16[512,1024]{1,0:T(8,128)(2,1)} %param.15) | data formatting | bytes 2097152 | tf_op args[1]
  40.0 1.7 %reshape.130 = f32[4,128,16,64]{1,0,3,2:T(4,128)} reshape(bf16[512,1024]{0,1:T(8,128)(2,1)S(1)} %copy.91) | data formatting | bytes 3145728 | tf_op jit(solution)/shard_map/convert_element_type | solution.py:140
  41.7 0.6 dynamic-slice
  43.0 0.1 compare_and_fusion
  43.2 0.2 fusion.45
  43.4 0.2 dynamic-update-slice
  43.7 9.6 %all-reduce = bf16[64]{0:T(256)(128)(2,1)S(1)} all-reduce(bf16[64]{0:T(256)(128)(2,1)S(1)} %dynamic-update-slice), channel_id=2, replica_groups=mesh['seq'=4,'head'=8] {'seq'}, use_global_device_ids=true, to_apply=%add | all-reduce | flops 64 | bytes 256
  53.3 0.1 reshape.131
  53.4 3.2 %fusion.4 = f32[4,16,64,128]{3,2,1,0:T(8,128)} fusion(f32[4,16,128]{2,1,0:T(8,128)S(1)} %bitcast_bitcast_fusion.1, f32[4,16,128]{2,1,0:T(8,128)S(1)} %reduce_window_sum.11, f32[4,128,128]{2,1,0:T(8,128)S(1)} %fusion.45, pred[4,128,128]{2,1,0:T(8,128)(4,1)S(1)} %compare_and_fusion, bf16[4,128,16,64]{1,0,3,2:T(4,128)(2,1)S(1)} %copy-done.3), kind=kOutput, calls=%fused_computation.13 | convolution fusion | flops 140509184 | bytes 3538944 | tf_op jit(solution)/shard_map/chts,cshp->cthp/dot_general | solution.py:94
  56.5 8.7 %all-gather.4.cloned.1.call-done = bf16[64,64,128]{2,1,0:T(8,128)(2,1)} async-done(((bf16[16,64,128]{2,1,0:T(8,128)(2,1)}), bf16[64,64,128]{2,1,0:T(8,128)(2,1)}) %all-gather.4.cloned.1.call-update) | async-done | bytes 1048592 | tf_op jit(solution)/shard_map/all_gather | solution.py:23
  65.2 4.5 %while.32 = (s32[]{:T(128)}, f32[16,64,128]{2,1,0:T(8,128)S(1)}, s32[]{:T(128)}, bf16[4,16]{1,0:T(4,128)(2,1)S(1)}, bf16[4,16,64,128]{3,2,1,0:T(8,128)(2,1)}, /*index=5*/s32[]{:T(128)}, s32[]{:T(128)}) while((s32[]{:T(128)}, f32[16,64,128]{2,1,0:T(8,128)S(1)}, s32[]{:T(128)}, bf16[4,16]{1,0:T(4,128)(2,1)S(1)}, ...), condition=%wide.region_4.5_spmd.clone, body=%wide.region_3.4_spmd.clone.sunk | while | flops 655380 | bytes 1310985 | solution.py:36
  65.3 1.1 %fusion.56 = f32[16,64,128]{2,1,0:T(8,128)S(1)} fusion(f32[16,64,128]{2,1,0:T(8,128)S(1)} %get-tuple-element.359, bf16[4,16,64,128]{3,2,1,0:T(8,128)(2,1)} %get-tuple-element.369, s32[]{:T(128)} %get-tuple-element.358, f32[16]{0:T(128)S(1)} %bitcast_convert_fusion.2, pred[]{:T(512)S(6)} %compare.9, pred[]{:T(512)S(6)} %lt.37), kind=kLoop, calls=%fused_computation.8.clone.1 | loop fusion | flops 655360 | bytes 1310790 | tf_op jit(solution)/shard_map/while/body/eval_jaxpr/jit(_where)/select_n | solution.py:34
  66.4 1.1 %fusion.56 = f32[16,64,128]{2,1,0:T(8,128)S(1)} fusion(f32[16,64,128]{2,1,0:T(8,128)S(1)} %get-tuple-element.359, bf16[4,16,64,128]{3,2,1,0:T(8,128)(2,1)} %get-tuple-element.369, s32[]{:T(128)} %get-tuple-element.358, f32[16]{0:T(128)S(1)} %bitcast_convert_fusion.2, pred[]{:T(512)S(6)} %compare.9, pred[]{:T(512)S(6)} %lt.37), kind=kLoop, calls=%fused_computation.8.clone.1 | loop fusion | flops 655360 | bytes 1310790 | tf_op jit(solution)/shard_map/while/body/eval_jaxpr/jit(_where)/select_n | solution.py:34
  67.5 1.1 %fusion.56 = f32[16,64,128]{2,1,0:T(8,128)S(1)} fusion(f32[16,64,128]{2,1,0:T(8,128)S(1)} %get-tuple-element.359, bf16[4,16,64,128]{3,2,1,0:T(8,128)(2,1)} %get-tuple-element.369, s32[]{:T(128)} %get-tuple-element.358, f32[16]{0:T(128)S(1)} %bitcast_convert_fusion.2, pred[]{:T(512)S(6)} %compare.9, pred[]{:T(512)S(6)} %lt.37), kind=kLoop, calls=%fused_computation.8.clone.1 | loop fusion | flops 655360 | bytes 1310790 | tf_op jit(solution)/shard_map/while/body/eval_jaxpr/jit(_where)/select_n | solution.py:34
  68.6 1.1 %fusion.56 = f32[16,64,128]{2,1,0:T(8,128)S(1)} fusion(f32[16,64,128]{2,1,0:T(8,128)S(1)} %get-tuple-element.359, bf16[4,16,64,128]{3,2,1,0:T(8,128)(2,1)} %get-tuple-element.369, s32[]{:T(128)} %get-tuple-element.358, f32[16]{0:T(128)S(1)} %bitcast_convert_fusion.2, pred[]{:T(512)S(6)} %compare.9, pred[]{:T(512)S(6)} %lt.37), kind=kLoop, calls=%fused_computation.8.clone.1 | loop fusion | flops 655360 | bytes 1310790 | tf_op jit(solution)/shard_map/while/body/eval_jaxpr/jit(_where)/select_n | solution.py:34
  69.8 6.2 %fusion.9 = (f32[4,128]{1,0:T(4,128)S(1)}, f32[4,128,16,64]{1,3,2,0:T(8,128)}) fusion(f32[4,128,16,64]{1,0,3,2:T(4,128)} %reshape.130, f32[16]{0:T(128)S(1)} %copy-done.7, bf16[4,128,16,64]{1,0,3,2:T(4,128)(2,1)S(1)} %copy-done.3, f32[4,128,16]{1,2,0:T(8,128)S(1)} %multiply_bitcast_fusion, bf16[4,128,128,1]{2,1,3,0:T(8,128)(2,1)S(1)} %bitcast.108, ...), kind=kOutput, calls=%fused_computation.18 | convolution fusion | flops 812645888 | bytes 10127680 | tf_op jit(solution)/shard_map/ctn,chpn->cthp/dot_general | solution.py:132
  76.0 0.6 stack.3
  76.6 3.7 %all-to-all-start = ((f32[8,1,512]{2,1,0:T(1,128)}), f32[8,1,512]{2,1,0:T(1,128)S(1)}, u32[]{:S(2)}, u32[]{:S(2)}) async-start(f32[8,1,512]{2,1,0:T(1,128)} %stack.3), calls=%async_computation | async-start | bytes 32768 | tf_op jit(solution)/shard_map/all_to_all | solution.py:143
  80.2 0.1 mul.327
  80.3 0.1 mul.328
  80.4 4.4 %copy.90 = f32[4,128,16,64]{1,0,3,2:T(4,128)} copy(f32[4,128,16,64]{1,3,2,0:T(8,128)} %get-tuple-element.243) | data formatting | bytes 4194304 | tf_op jit(solution)/shard_map/add | solution.py:136
  84.8 0.2 all-to-all-done
  85.1 2.5 %fusion.13 = bf16[512,1024]{0,1:T(8,128)(2,1)S(1)} fusion(f32[128,8,4,128]{3,2,1,0:T(4,128)} %bitcast.103, bf16[512,1024]{0,1:T(8,128)(2,1)S(1)} %copy-done.2, f32[1024]{0:T(1024)S(1)} %copy-done.6, f32[512]{0:T(512)S(1)} %add_rsqrt_fusion, f32[1024]{0:T(1024)S(1)} %mul.328, bf16[512,1024]{0,1:T(8,128)(2,1)S(1)} %copy.91), kind=kLoop, calls=%fused_computation.23 | loop fusion | flops 6291456 | bytes 5253120 | tf_op jit(solution)/shard_map/convert_element_type | solution.py:150
  87.5 1.3 %copy.95 = bf16[512,1024]{1,0:T(8,128)(2,1)} copy(bf16[512,1024]{0,1:T(8,128)(2,1)S(1)} %fusion.13) | data formatting | bytes 2097152 | tf_op jit(solution)/shard_map/convert_element_type | solution.py:150
  (52 shorter events, 0.5 us)
Async XLA Ops:
  6.5 17.3 %copy-start = (f32[16,512]{1,0:T(8,128)S(1)}, f32[16,512]{1,0:T(8,128)}, u32[]{:S(2)}) copy-start(f32[16,512]{1,0:T(8,128)} %param.19) | copy-start | bytes 98308
  6.5 18.8 %copy-start.4 = (s32[512]{0:T(512)S(1)}, s32[512]{0:T(512)}, u32[]{:S(2)}) copy-start(s32[512]{0:T(512)} %param.23) | copy-start | bytes 6148
  6.5 17.1 %copy-start.5 = (f32[4,1024]{1,0:T(4,128)S(1)}, f32[4,1024]{1,0:T(4,128)}, u32[]{:S(2)}) copy-start(f32[4,1024]{1,0:T(4,128)} %param.17) | copy-start | bytes 49156
  6.5 17.1 %copy-start.8 = (f32[16]{0:T(128)S(1)}, f32[16]{0:T(128)}, u32[]{:S(2)}) copy-start(f32[16]{0:T(128)} %param.20) | copy-start | bytes 196
  6.5 58.7 %all-gather.4.cloned.1.call-start = ((), (), s32[]{:S(2)}) async-start(), calls=%async_computation.1 | async-start | bytes 1310720 | tf_op jit(solution)/shard_map/all_gather | solution.py:23
  7.6 19.5 %collective-permute-start.2 = (bf16[3,256]{1,0:T(4,128)(2,1)S(1)}, bf16[3,256]{1,0:T(4,128)(2,1)S(1)}, u32[]{:S(2)}, u32[]{:S(2)}) collective-permute-start(bf16[3,256]{1,0:T(4,128)(2,1)S(1)} %fusion.36), channel_id=1, source_target_pairs={{0,8},{8,16},{16,24},{1,9},{9,17},{17,25},{2,10},{10,18},{18,26},{... | collective-permute-start | bytes 4616 | tf_op jit(solution)/shard_map/ppermute | solution.py:17
  13.4 11.8 %collective-permute-start = (bf16[3]{0:T(256)(128)(2,1)S(1)}, bf16[3]{0:T(256)(128)(2,1)S(1)}, u32[]{:S(2)}, u32[]{:S(2)}) collective-permute-start(bf16[3]{0:T(256)(128)(2,1)S(1)} %slice.84), channel_id=1, source_target_pairs={{0,8},{8,16},{16,24},{1,9},{9,17},{17,25},{2,10},{10,18},{18,26},{... | collective-permute-start | bytes 26 | tf_op jit(solution)/shard_map/ppermute | solution.py:17
  17.8 10.1 %collective-permute-start.1 = (bf16[3,1024]{0,1:T(8,128)(2,1)S(1)}, bf16[3,1024]{0,1:T(8,128)(2,1)S(1)}, u32[]{:S(2)}, u32[]{:S(2)}) collective-permute-start(bf16[3,1024]{0,1:T(8,128)(2,1)S(1)} %copy.83), channel_id=1, source_target_pairs={{0,8},{8,16},{16,24},{1,9},{9,17},{17,25},{2,10},{10,18},{18,26},{... | collective-permute-start | bytes 18440 | tf_op jit(solution)/shard_map/ppermute | solution.py:17
  30.6 1.3 %copy-start.1 = (bf16[512,1024]{0,1:T(8,128)(2,1)}, bf16[512,1024]{0,1:T(8,128)(2,1)S(1)}, u32[]{:S(2)}) copy-start(bf16[512,1024]{0,1:T(8,128)(2,1)S(1)} %multiply_convert_fusion.2) | copy-start | bytes 3145732
  40.0 1.7 %copy-start.9 = (u32[32]{0:T(128)S(1)}, u32[32]{0:T(128)}, u32[]{:S(2)}) copy-start(u32[32]{0:T(128)} %constant.97) | copy-start | bytes 388
  40.0 13.4 %copy-start.3 = (bf16[4,128,16,64]{1,0,3,2:T(4,128)(2,1)S(1)}, bf16[4,128,16,64]{1,0,3,2:T(4,128)(2,1)}, u32[]{:S(2)}) copy-start(bf16[4,128,16,64]{1,0,3,2:T(4,128)(2,1)} %reshape.122) | copy-start | bytes 3145732
  65.2 4.5 %copy-start.7 = (f32[16]{0:T(128)S(1)}, f32[16]{0:T(128)}, u32[]{:S(2)}) copy-start(f32[16]{0:T(128)} %param.21) | copy-start | bytes 196
  76.6 8.4 %all-to-all-start = ((f32[8,1,512]{2,1,0:T(1,128)}), f32[8,1,512]{2,1,0:T(1,128)S(1)}, u32[]{:S(2)}, u32[]{:S(2)}) async-start(f32[8,1,512]{2,1,0:T(1,128)} %stack.3), calls=%async_computation | async-start | bytes 32768 | tf_op jit(solution)/shard_map/all_to_all | solution.py:143
  80.4 4.7 %copy-start.2 = (bf16[512,1024]{0,1:T(8,128)(2,1)S(1)}, bf16[512,1024]{0,1:T(8,128)(2,1)}, u32[]{:S(2)}) copy-start(bf16[512,1024]{0,1:T(8,128)(2,1)} %copy-done.1) | copy-start | bytes 3145732
  80.4 4.7 %copy-start.6 = (f32[1024]{0:T(1024)S(1)}, f32[1024]{0:T(1024)}, u32[]{:S(2)}) copy-start(f32[1024]{0:T(1024)} %param.22) | copy-start | bytes 12292
Sparse Core Ops, SparseCore 0:
  38.6 26.6 all-gather.3
